TPU v7x, 128 devices: a whole 4x4x4 slice. The times are simulated.
128 devices in a mesh: pix: 32 (over y, z, core), freq: 4 (over x).
Axes of the slice: x: 4, y: 4, z: 4, core: 2. Of those that a mesh axis runs over, the one named last changes fastest.
Arguments:
- cube: float32 [1024, 65536], P('freq', 'pix'), may hold values from -6 to 6
- probes: float32 [32, 65536], P(None, 'pix'), may hold values from -6 to 6
- galaxy: float32 [65536], P('pix'), may hold values from -6 to 6
- slices: int32 [65536], P('pix'), may hold values from 0 to 127
- valid: int32 [65536], P('pix'), may hold values 0 or 1
Outputs:
- cleaned: float32 [1024, 65536], P('freq', 'pix')
- cross: float32 [1024, 128], P('freq')
All inputs are finite; a program needn't handle non-finite values. No bound on the sum of `valid` on one device may be relied on, other than what follows from the above.
Results may differ from a plain program's by a relative error of at most 0.00019.
Values sent between devices are 32-bit elements; how exact they have to be, the bound alone decides.
No kernel may reach another device: no remote copies, remote signals or barrier semaphores. Data moves between devices by JAX's collectives and lax.ppermute only.
A program may use at most 64 MiB of HBM per device.

v0:
```python
import jax
import jax.numpy as jnp
from jax import lax
from jax.sharding import PartitionSpec as P

NS = 128
ITERS = 4


def prefix(value, axis, join, neutral):
    count, mine = (lax.axis_size(axis), lax.axis_index(axis))
    pieces = lax.all_gather(value, axis)
    total = jnp.full_like(value, 0) + jnp.asarray(neutral, value.dtype)

    def lap(position, total):
        longer = join(total, pieces[position])
        return jnp.where(position < mine, longer, total)

    return lax.fori_loop(0, count - 1, lap, total)


def broadcast(value, axis, source):
    kept = jnp.where(lax.axis_index(axis) == source, value, 0).astype(value.dtype)
    return lax.psum(kept, axis)


def multiply(left, right):
    return jnp.dot(left, right, precision=lax.Precision.HIGHEST, preferred_element_type=jnp.float32)


def orthonormal(factor):
    gram = multiply(factor.T, factor)
    lower = jnp.linalg.cholesky(gram)
    return lax.linalg.triangular_solve(lower, factor, left_side=False, lower=True, transpose_a=True)


def combine_add(earlier, later):
    return earlier + later


def total_pix(term):
    before = prefix(term, "pix", combine_add, jnp.zeros_like(term))
    return broadcast(before + term, "pix", lax.axis_size("pix") - 1)


def fold_freq(term):
    return lax.psum_scatter(term, "freq", scatter_dimension=0, tiled=True)


def gather_rows(term):
    return lax.all_gather(term, "freq", axis=0, tiled=True)


def slice_table(slices, weights):
    levels = jnp.arange(NS, dtype=jnp.int32)
    return (slices[:, None] == levels[None, :]).astype(jnp.float32) * weights[:, None]


def body(cube, probes, galaxy, slices, valid):
    pixels = lax.axis_size("pix") * cube.shape[1]
    factor_scale = (float(pixels) / float(NS)) ** (-0.5)
    weights = galaxy * valid.astype(jnp.float32)
    own = lax.axis_index("freq")
    local = lax.all_to_all(cube, "freq", split_axis=1, concat_axis=0, tiled=True)
    width = local.shape[1]
    start = own * width
    probe_cols = lax.dynamic_slice_in_dim(probes, start, width, 1)
    own_weights = lax.dynamic_slice_in_dim(weights, start, width, 0)
    own_slices = lax.dynamic_slice_in_dim(slices, start, width, 0)
    basis = orthonormal(gather_rows(total_pix(fold_freq(multiply(local, probe_cols.T)))))
    for step in range(ITERS):
        amps = multiply(basis.T, local)
        basis = orthonormal(gather_rows(total_pix(fold_freq(multiply(local, amps.T)))))
    amps = multiply(basis.T, local)
    cleaned_local = local - multiply(basis, amps)
    table = slice_table(own_slices, own_weights)
    cross = total_pix(fold_freq(multiply(cleaned_local, table))) * factor_scale
    cleaned = lax.all_to_all(cleaned_local, "freq", split_axis=0, concat_axis=1, tiled=True)
    return (cleaned, cross)


def solution(mesh):
    in_specs = (P("freq", "pix"), P(None, "pix"), P("pix"), P("pix"), P("pix"))
    out_specs = (P("freq", "pix"), P("freq", None))
    return jax.shard_map(body, mesh=mesh, in_specs=in_specs, out_specs=out_specs, check_vma=False)
```

profile of v0, /device:TPU:0, one launch (start us, length us, event | category | flops | bytes accessed | tf_op | source)
XLA Modules:
  0.0 1481.6 jit_solution(6170851042177497390)
XLA Ops:
  7.2 3.2 copy.32
  10.4 4.4 all-to-all-start
  14.8 26.3 %all-to-all-done = f32[256,4,512]{2,0,1:T(8,128)S(1)} async-done(((f32[256,4,512]{2,0,1:T(8,128)}), f32[256,4,512]{2,0,1:T(8,128)S(1)}, u32[]{:S(2)}, u32[]{:S(2)}) %all-to-all-start) | async-done | bytes 2097184 | tf_op jit(solution)/shard_map/all_to_all | solution.py:64
  41.1 2.7 convolution_bitcast_fusion.9
  43.8 21.2 %reduce-scatter.7.cloned.1.call-done = f32[256,32]{0,1:T(8,128)} async-done(((f32[1024,32]{0,1:T(8,128)}), f32[256,32]{0,1:T(8,128)}) %reduce-scatter.7.cloned.1.call-update) | async-done | bytes 32784 | tf_op jit(solution)/shard_map/reduce_scatter | solution.py:47
  65.2 44.9 %all-gather.13.cloned.1.call-done = f32[8192,32]{0,1:T(8,128)} async-done(((f32[256,32]{0,1:T(8,128)}), f32[8192,32]{0,1:T(8,128)}) %all-gather.13.cloned.1.call-update) | async-done | bytes 1048592 | tf_op jit(solution)/shard_map/all_gather | solution.py:12
  110.0 3.6 copy.24
  113.6 30.1 %while.84 = (s32[]{:T(128)}, f32[256,32]{1,0:T(8,128)S(1)}, s32[]{:T(128)}, f32[32,256,32]{2,1,0:T(8,128)}, s32[]{:T(128)}, /*index=5*/s32[]{:T(128)}) while((s32[]{:T(128)}, f32[256,32]{1,0:T(8,128)S(1)}, s32[]{:T(128)}, f32[32,256,32]{2,1,0:T(8,128)}, s32[]{:T(128)}, /*index=5*/s32[]{:T(128)}) %tuple.222), condition=%wide.region_2.3_spmd.clone, body=%wide.region_1.2_spmd.clone.sunk | while | flops 24580 | bytes 98397 | solution.py:19
  143.8 126.2 %psum.42 = f32[256,32]{0,1:T(8,128)S(1)} all-reduce(f32[256,32]{0,1:T(8,128)S(1)} %add_select_fusion.11), channel_id=1, replica_groups=mesh['pix'=32,'freq'=4] {'pix'}, use_global_device_ids=true, to_apply=%region_3.4 | all-reduce | flops 8192 | bytes 65536 | tf_op jit(solution)/shard_map/psum | solution.py:24
  270.0 12.3 all_gather.53
  282.6 2.9 cholesky.89
  291.0 2.7 convolution_bitcast_fusion.7
  293.7 16.4 %reduce-scatter.9.cloned.1.call-done = f32[256,32]{0,1:T(8,128)} async-done(((f32[1024,32]{0,1:T(8,128)}), f32[256,32]{0,1:T(8,128)}) %reduce-scatter.9.cloned.1.call-update) | async-done | bytes 32784 | tf_op jit(solution)/shard_map/reduce_scatter | solution.py:47
  310.1 44.7 %all-gather.15.cloned.1.call-done = f32[8192,32]{0,1:T(8,128)} async-done(((f32[256,32]{0,1:T(8,128)}), f32[8192,32]{0,1:T(8,128)}) %all-gather.15.cloned.1.call-update) | async-done | bytes 1048592 | tf_op jit(solution)/shard_map/all_gather | solution.py:12
  354.9 3.6 copy.25
  358.4 30.1 %while.85 = (s32[]{:T(128)}, f32[256,32]{1,0:T(8,128)S(1)}, s32[]{:T(128)}, f32[32,256,32]{2,1,0:T(8,128)}, s32[]{:T(128)}, /*index=5*/s32[]{:T(128)}) while((s32[]{:T(128)}, f32[256,32]{1,0:T(8,128)S(1)}, s32[]{:T(128)}, f32[32,256,32]{2,1,0:T(8,128)}, s32[]{:T(128)}, /*index=5*/s32[]{:T(128)}) %tuple.223), condition=%wide.region_8.11_spmd.clone, body=%wide.region_7.10_spmd.clone.sunk | while | flops 24580 | bytes 98397 | solution.py:19
  388.6 126.2 %psum.43 = f32[256,32]{0,1:T(8,128)S(1)} all-reduce(f32[256,32]{0,1:T(8,128)S(1)} %add_select_fusion.10), channel_id=1, replica_groups=mesh['pix'=32,'freq'=4] {'pix'}, use_global_device_ids=true, to_apply=%region_9.12 | all-reduce | flops 8192 | bytes 65536 | tf_op jit(solution)/shard_map/psum | solution.py:24
  514.8 12.3 all_gather.56
  527.4 2.9 cholesky.100
  535.8 2.7 convolution_bitcast_fusion.5
  538.5 16.4 %reduce-scatter.11.cloned.1.call-done = f32[256,32]{0,1:T(8,128)} async-done(((f32[1024,32]{0,1:T(8,128)}), f32[256,32]{0,1:T(8,128)}) %reduce-scatter.11.cloned.1.call-update) | async-done | bytes 32784 | tf_op jit(solution)/shard_map/reduce_scatter | solution.py:47
  555.0 44.7 %all-gather.17.cloned.1.call-done = f32[8192,32]{0,1:T(8,128)} async-done(((f32[256,32]{0,1:T(8,128)}), f32[8192,32]{0,1:T(8,128)}) %all-gather.17.cloned.1.call-update) | async-done | bytes 1048592 | tf_op jit(solution)/shard_map/all_gather | solution.py:12
  599.7 3.6 copy.26
  603.3 30.1 %while.86 = (s32[]{:T(128)}, f32[256,32]{1,0:T(8,128)S(1)}, s32[]{:T(128)}, f32[32,256,32]{2,1,0:T(8,128)}, s32[]{:T(128)}, /*index=5*/s32[]{:T(128)}) while((s32[]{:T(128)}, f32[256,32]{1,0:T(8,128)S(1)}, s32[]{:T(128)}, f32[32,256,32]{2,1,0:T(8,128)}, s32[]{:T(128)}, /*index=5*/s32[]{:T(128)}) %tuple.224), condition=%wide.region_12.15_spmd.clone, body=%wide.region_11.14_spmd.clone.sunk | while | flops 24580 | bytes 98397 | solution.py:19
  633.4 126.2 %psum.44 = f32[256,32]{0,1:T(8,128)S(1)} all-reduce(f32[256,32]{0,1:T(8,128)S(1)} %add_select_fusion.9), channel_id=1, replica_groups=mesh['pix'=32,'freq'=4] {'pix'}, use_global_device_ids=true, to_apply=%region_13.16 | all-reduce | flops 8192 | bytes 65536 | tf_op jit(solution)/shard_map/psum | solution.py:24
  759.6 12.5 all_gather.59
  772.4 2.9 cholesky.111
  780.8 2.7 convolution_bitcast_fusion.3
  783.5 16.4 %reduce-scatter.13.cloned.1.call-done = f32[256,32]{0,1:T(8,128)} async-done(((f32[1024,32]{0,1:T(8,128)}), f32[256,32]{0,1:T(8,128)}) %reduce-scatter.13.cloned.1.call-update) | async-done | bytes 32784 | tf_op jit(solution)/shard_map/reduce_scatter | solution.py:47
  800.0 44.8 %all-gather.19.cloned.1.call-done = f32[8192,32]{0,1:T(8,128)} async-done(((f32[256,32]{0,1:T(8,128)}), f32[8192,32]{0,1:T(8,128)}) %all-gather.19.cloned.1.call-update) | async-done | bytes 1048592 | tf_op jit(solution)/shard_map/all_gather | solution.py:12
  844.8 3.6 copy.27
  848.4 30.1 %while.87 = (s32[]{:T(128)}, f32[256,32]{1,0:T(8,128)S(1)}, s32[]{:T(128)}, f32[32,256,32]{2,1,0:T(8,128)}, s32[]{:T(128)}, /*index=5*/s32[]{:T(128)}) while((s32[]{:T(128)}, f32[256,32]{1,0:T(8,128)S(1)}, s32[]{:T(128)}, f32[32,256,32]{2,1,0:T(8,128)}, s32[]{:T(128)}, /*index=5*/s32[]{:T(128)}) %tuple.225), condition=%wide.region_16.19_spmd.clone, body=%wide.region_15.18_spmd.clone.sunk | while | flops 24580 | bytes 98397 | solution.py:19
  878.5 126.2 %psum.45 = f32[256,32]{0,1:T(8,128)S(1)} all-reduce(f32[256,32]{0,1:T(8,128)S(1)} %add_select_fusion.8), channel_id=1, replica_groups=mesh['pix'=32,'freq'=4] {'pix'}, use_global_device_ids=true, to_apply=%region_17.20 | all-reduce | flops 8192 | bytes 65536 | tf_op jit(solution)/shard_map/psum | solution.py:24
  1004.8 12.3 all_gather.62
  1017.4 2.9 cholesky.122
  1028.5 16.4 %reduce-scatter.15.cloned.1.call-done = f32[256,32]{0,1:T(8,128)} async-done(((f32[1024,32]{0,1:T(8,128)}), f32[256,32]{0,1:T(8,128)}) %reduce-scatter.15.cloned.1.call-update) | async-done | bytes 32784 | tf_op jit(solution)/shard_map/reduce_scatter | solution.py:47
  1046.5 43.1 %all-gather.21.cloned.1.call-done = f32[8192,32]{0,1:T(8,128)} async-done(((f32[256,32]{0,1:T(8,128)}), f32[8192,32]{0,1:T(8,128)}) %all-gather.21.cloned.1.call-update) | async-done | bytes 1048592 | tf_op jit(solution)/shard_map/all_gather | solution.py:12
  1089.6 3.6 copy.28
  1093.2 30.1 %while.88 = (s32[]{:T(128)}, f32[256,32]{1,0:T(8,128)S(1)}, s32[]{:T(128)}, f32[32,256,32]{2,1,0:T(8,128)}, s32[]{:T(128)}, /*index=5*/s32[]{:T(128)}) while((s32[]{:T(128)}, f32[256,32]{1,0:T(8,128)S(1)}, s32[]{:T(128)}, f32[32,256,32]{2,1,0:T(8,128)}, s32[]{:T(128)}, /*index=5*/s32[]{:T(128)}) %tuple.226), condition=%wide.region_20.23_spmd.clone, body=%wide.region_19.22_spmd.clone.sunk | while | flops 24580 | bytes 98397 | solution.py:19
  1123.3 126.2 %psum.46 = f32[256,32]{0,1:T(8,128)S(1)} all-reduce(f32[256,32]{0,1:T(8,128)S(1)} %add_select_fusion.7), channel_id=1, replica_groups=mesh['pix'=32,'freq'=4] {'pix'}, use_global_device_ids=true, to_apply=%region_21.24 | all-reduce | flops 8192 | bytes 65536 | tf_op jit(solution)/shard_map/psum | solution.py:24
  1249.6 12.5 all_gather.65
  1262.4 2.9 cholesky.133
  1273.9 2.7 fusion
  1276.7 17.3 %reduce-scatter.17.cloned.1.call-done = f32[256,128]{1,0:T(8,128)} async-done(((f32[1024,128]{1,0:T(8,128)}), f32[256,128]{1,0:T(8,128)}) %reduce-scatter.17.cloned.1.call-update) | async-done | bytes 131088 | tf_op jit(solution)/shard_map/reduce_scatter | solution.py:47
  1294.1 3.6 all-to-all-start.1
  1297.7 44.4 %all-gather.23.cloned.1.call-done = f32[8192,128]{1,0:T(8,128)} async-done(((f32[256,128]{1,0:T(8,128)}), f32[8192,128]{1,0:T(8,128)}) %all-gather.23.cloned.1.call-update) | async-done | bytes 4194320 | tf_op jit(solution)/shard_map/all_gather | solution.py:12
  1342.2 30.0 %while.89 = (s32[]{:T(128)}, f32[256,128]{1,0:T(8,128)S(1)}, s32[]{:T(128)}, f32[32,256,128]{2,1,0:T(8,128)}, s32[]{:T(128)}, /*index=5*/s32[]{:T(128)}) while((s32[]{:T(128)}, f32[256,128]{1,0:T(8,128)S(1)}, s32[]{:T(128)}, f32[32,256,128]{2,1,0:T(8,128)}, s32[]{:T(128)}, /*index=5*/s32[]{:T(128)}) %tuple.227), condition=%wide.region_24.27_spmd.clone, body=%wide.region_23.26_spmd.clone.sunk | while | flops 98308 | bytes 393309 | solution.py:19
  1374.5 99.0 %all-reduce.2.cloned.1.call-done = f32[256,128]{1,0:T(8,128)} async-done(((f32[256,128]{1,0:T(8,128)}), f32[256,128]{1,0:T(8,128)}) %all-reduce.2.cloned.1.call-update) | async-done | bytes 131088 | tf_op jit(solution)/shard_map/psum | solution.py:24
  (297 shorter events, 217.1 us)
Async XLA Ops:
  7.2 33.9 %copy-start = (f32[32,2048]{1,0:T(8,128)S(1)}, f32[32,2048]{1,0:T(8,128)}, u32[]{:S(2)}) copy-start(f32[32,2048]{1,0:T(8,128)} %param.21) | copy-start | bytes 786436
  10.4 30.7 %all-to-all-start = ((f32[256,4,512]{2,0,1:T(8,128)}), f32[256,4,512]{2,0,1:T(8,128)S(1)}, u32[]{:S(2)}, u32[]{:S(2)}) async-start(f32[256,4,512]{2,0,1:T(8,128)} %bitcast.156), calls=%async_computation | async-start | bytes 4194304 | tf_op jit(solution)/shard_map/all_to_all | solution.py:64
  14.8 50.3 %reduce-scatter.7.cloned.1.call-start = ((), (), s32[]{:S(2)}) async-start(), calls=%async_computation.8 | async-start | bytes 163840 | tf_op jit(solution)/shard_map/reduce_scatter | solution.py:47
  43.8 66.3 %all-gather.13.cloned.1.call-start = ((), (), s32[]{:S(2)}) async-start(), calls=%async_computation.15 | async-start | bytes 1081344 | tf_op jit(solution)/shard_map/all_gather | solution.py:12
  65.1 245.0 %reduce-scatter.9.cloned.1.call-start = ((), (), s32[]{:S(2)}) async-start(), calls=%async_computation.9 | async-start | bytes 163840 | tf_op jit(solution)/shard_map/reduce_scatter | solution.py:47
  113.6 30.1 %copy-start.3 = (f32[256,32]{0,1:T(8,128)S(1)}, f32[256,32]{0,1:T(8,128)}, u32[]{:S(2)}) copy-start(f32[256,32]{0,1:T(8,128)} %reduce-scatter.7.cloned.1.call-done) | copy-start | bytes 98308
  293.7 61.2 %all-gather.15.cloned.1.call-start = ((), (), s32[]{:S(2)}) async-start(), calls=%async_computation.16 | async-start | bytes 1081344 | tf_op jit(solution)/shard_map/all_gather | solution.py:12
  310.1 244.8 %reduce-scatter.11.cloned.1.call-start = ((), (), s32[]{:S(2)}) async-start(), calls=%async_computation.10 | async-start | bytes 163840 | tf_op jit(solution)/shard_map/reduce_scatter | solution.py:47
  358.4 30.1 %copy-start.5 = (f32[256,32]{0,1:T(8,128)S(1)}, f32[256,32]{0,1:T(8,128)}, u32[]{:S(2)}) copy-start(f32[256,32]{0,1:T(8,128)} %reduce-scatter.9.cloned.1.call-done) | copy-start | bytes 98308
  538.5 61.2 %all-gather.17.cloned.1.call-start = ((), (), s32[]{:S(2)}) async-start(), calls=%async_computation.17 | async-start | bytes 1081344 | tf_op jit(solution)/shard_map/all_gather | solution.py:12
  554.9 245.0 %reduce-scatter.13.cloned.1.call-start = ((), (), s32[]{:S(2)}) async-start(), calls=%async_computation.11 | async-start | bytes 163840 | tf_op jit(solution)/shard_map/reduce_scatter | solution.py:47
  603.2 30.1 %copy-start.6 = (f32[256,32]{0,1:T(8,128)S(1)}, f32[256,32]{0,1:T(8,128)}, u32[]{:S(2)}) copy-start(f32[256,32]{0,1:T(8,128)} %reduce-scatter.11.cloned.1.call-done) | copy-start | bytes 98308
  783.5 61.3 %all-gather.19.cloned.1.call-start = ((), (), s32[]{:S(2)}) async-start(), calls=%async_computation.18 | async-start | bytes 1081344 | tf_op jit(solution)/shard_map/all_gather | solution.py:12
  799.9 244.9 %reduce-scatter.15.cloned.1.call-start = ((), (), s32[]{:S(2)}) async-start(), calls=%async_computation.12 | async-start | bytes 163840 | tf_op jit(solution)/shard_map/reduce_scatter | solution.py:47
  848.4 30.1 %copy-start.7 = (f32[256,32]{0,1:T(8,128)S(1)}, f32[256,32]{0,1:T(8,128)}, u32[]{:S(2)}) copy-start(f32[256,32]{0,1:T(8,128)} %reduce-scatter.13.cloned.1.call-done) | copy-start | bytes 98308
  1028.4 61.2 %all-gather.21.cloned.1.call-start = ((), (), s32[]{:S(2)}) async-start(), calls=%async_computation.19 | async-start | bytes 1081344 | tf_op jit(solution)/shard_map/all_gather | solution.py:12
  1044.9 249.2 %reduce-scatter.17.cloned.1.call-start = ((), (), s32[]{:S(2)}) async-start(), calls=%async_computation.13 | async-start | bytes 655360 | tf_op jit(solution)/shard_map/reduce_scatter | solution.py:47
  1093.2 30.1 %copy-start.4 = (f32[256,32]{0,1:T(8,128)S(1)}, f32[256,32]{0,1:T(8,128)}, u32[]{:S(2)}) copy-start(f32[256,32]{0,1:T(8,128)} %reduce-scatter.15.cloned.1.call-done) | copy-start | bytes 98308
  1272.6 1.3 copy-start.1
  1276.6 65.5 %all-gather.23.cloned.1.call-start = ((), (), s32[]{:S(2)}) async-start(), calls=%async_computation.20 | async-start | bytes 4325376 | tf_op jit(solution)/shard_map/all_gather | solution.py:12
  1294.1 78.9 %all-to-all-start.1 = ((f32[4,256,512]{2,1,0:T(8,128)}), f32[4,256,512]{2,1,0:T(8,128)S(1)}, u32[]{:S(2)}, u32[]{:S(2)}) async-start(f32[4,256,512]{2,1,0:T(8,128)} %bitcast.154), calls=%async_computation.6 | async-start | bytes 4194304 | tf_op jit(solution)/shard_map/all_to_all | solution.py:78
  1297.7 74.5 %copy-start.2 = (f32[256,128]{1,0:T(8,128)S(1)}, f32[256,128]{1,0:T(8,128)}, u32[]{:S(2)}) copy-start(f32[256,128]{1,0:T(8,128)} %reduce-scatter.17.cloned.1.call-done) | copy-start | bytes 393220
  1297.7 175.8 %all-reduce.2.cloned.1.call-start = ((), (), s32[]{:S(2)}) async-start(), calls=%async_computation.14 | async-start | bytes 262144 | tf_op jit(solution)/shard_map/psum | solution.py:24
Sparse Core Ops, SparseCore 0:
  43.9 21.1 reduce-scatter.6
  67.2 42.7 all-gather.12
  293.8 16.2 reduce-scatter.8
  312.1 42.7 all-gather.14
  538.6 16.2 reduce-scatter.10
  556.9 42.7 all-gather.16
  783.6 16.2 reduce-scatter.12
  802.1 42.7 all-gather.18
  1028.5 16.2 reduce-scatter.14
  1046.9 42.6 all-gather.20
  1276.8 17.2 reduce-scatter.16
  1296.1 45.9 all-gather.22
  1373.0 100.4 all-reduce.1
where the time goes:
time: 1490 us; the launch traced here: 1480 us
  blocking collectives  693 us (47%)
  waiting for transfers between devices  496 us (33%)
  other arithmetic  213 us (14%)
  matrix products  27.2 us (2%)
  local copies, waits for them, and re-layouts  25.4 us (2%)
    psum x5, blocking collectives, broadcast(): return lax.psum(kept, axis)  631 us
    all_gather x6, waiting for transfers between devices, prefix(): pieces = lax.all_gather(value, axis)  267 us
    select_n x186, other arithmetic, lap(): return jnp.where(position < mine, longer, total)  176 us
    reduce_scatter x6, waiting for transfers between devices, fold_freq(): return lax.psum_scatter(term, 'freq', scatter_dimension=0, tiled=True)  104 us
    psum x1, waiting for transfers between devices, broadcast(): return lax.psum(kept, axis)  99 us
    all_gather x5, blocking collectives, gather_rows(): return lax.all_gather(term, 'freq', axis=0, tiled=True)  61.8 us
  transfers between devices with their start and end apart: 15, of which 14 were waited for; matrix products, arithmetic and copies ran while one was open for 2% of the time, Pallas kernels for 0%

commit v1 on v0

v1 whole, which is shorter than its diff:
```python
import functools

import jax
import jax.numpy as jnp
from jax import lax
from jax.experimental import pallas as pl
from jax.experimental.pallas import tpu as pltpu
from jax.sharding import Mesh, PartitionSpec as P

NS = 128
ITERS = 4
K = 32
T = 128
CHIPS = ("y", "z", "x")
HIGHEST = lax.Precision.HIGHEST
NN = (((1,), (0,)), ((), ()))
NT = (((1,), (1,)), ((), ()))
TN = (((0,), (0,)), ((), ()))


def multiply(left, right, dims=NN):
    return lax.dot_general(left, right, dims, precision=HIGHEST, preferred_element_type=jnp.float32)


def blocks_of(channels):
    count = channels // T
    return [(i, j) for i in range(count) for j in range(i, count)]


def rows_of(channels):
    gram = len(blocks_of(channels)) * T
    sketch = gram + K * channels // T
    return gram, sketch, sketch + channels


def gram_kernel(local_ref, probes_ref, weights_ref, slices_ref, out_ref):
    channels, width = local_ref.shape
    gram, sketch, total = rows_of(channels)
    position = {pair: index for index, pair in enumerate(blocks_of(channels))}
    step = 2 * T
    for top in range(0, channels, step):
        product = multiply(local_ref[top : top + step, :], local_ref[top:, :], NT)
        for half in range(2):
            i = top // T + half
            for j in range(i, channels // T):
                at = position[(i, j)] * T
                left = (j - top // T) * T
                out_ref[at : at + T, :] = product[half * T : half * T + T, left : left + T]
    sums = multiply(probes_ref[...], local_ref[...], NT)
    for j in range(channels // T):
        out_ref[gram + j * K : gram + (j + 1) * K, :] = sums[:, j * T : (j + 1) * T]
    levels = lax.broadcasted_iota(jnp.int32, (NS, width), 0)
    table = jnp.where(levels == slices_ref[...], weights_ref[...], 0.0)
    out_ref[sketch:total, :] = multiply(local_ref[...], table, NT)
    if total < out_ref.shape[0]:
        out_ref[total:, :] = jnp.zeros((out_ref.shape[0] - total, T), jnp.float32)


def orthonormal(factor):
    gram = multiply(factor, factor, NT)
    rows = lax.broadcasted_iota(jnp.int32, (K, T), 0)
    lanes = lax.broadcasted_iota(jnp.int32, (K, T), 1)
    unit = jnp.where(lanes == rows + K, 1.0, 0.0).astype(jnp.float32)
    wide = jnp.concatenate([gram, jnp.zeros((K, T - K), jnp.float32)], axis=1) + unit
    for k in range(K - 1):
        row = wide[k : k + 1, :]
        scaled = row / wide[k : k + 1, k : k + 1]
        column = jnp.where(rows[:, :1] > k, wide[:, k : k + 1], 0.0)
        wide = wide - column * scaled
    pivots = jnp.sum(jnp.where(lanes == rows, wide, 0.0), axis=1, keepdims=True)
    inverse = wide[:, K : 2 * K] * lax.rsqrt(pivots)
    return multiply(inverse, factor)


def iterate_kernel(scale, packed_ref, basis_ref, cross_ref, full):
    channels = basis_ref.shape[1]
    gram, sketch, total = rows_of(channels)
    for index, (i, j) in enumerate(blocks_of(channels)):
        block = packed_ref[index * T : (index + 1) * T, :]
        full[i * T : (i + 1) * T, j * T : (j + 1) * T] = block
        if i != j:
            full[j * T : (j + 1) * T, i * T : (i + 1) * T] = block.T
    factor = jnp.concatenate([packed_ref[gram + j * K : gram + (j + 1) * K, :] for j in range(channels // T)], axis=1)
    basis = orthonormal(factor)
    for step in range(ITERS):
        basis = orthonormal(multiply(basis, full[...]))
    basis_ref[...] = basis
    sums = packed_ref[sketch:total, :]
    inner = multiply(basis, sums)
    cross_ref[...] = (sums - multiply(basis, inner, TN)) * scale


def body(cube, probes, galaxy, slices, valid):
    nx, nc = lax.axis_size("x"), lax.axis_size("c")
    pixels = lax.axis_size("y") * lax.axis_size("z") * nc * cube.shape[1]
    scale = (float(pixels) / float(NS)) ** (-0.5)
    own, core = lax.axis_index("x"), lax.axis_index("c")
    rows, chips = cube.shape[0], lax.axis_size(CHIPS)
    channels = rows * nx
    local = lax.all_to_all(cube, "x", split_axis=1, concat_axis=0, tiled=True)
    width = local.shape[1]
    start = own * width
    weights = (galaxy * valid.astype(jnp.float32))[None, :]
    probe_cols = lax.dynamic_slice_in_dim(probes, start, width, 1)
    own_weights = lax.dynamic_slice_in_dim(weights, start, width, 1)
    own_slices = lax.dynamic_slice_in_dim(slices[None, :], start, width, 1)

    total = rows_of(channels)[2]
    piece = -(-total // (nc * chips * 8)) * 8
    packed = pl.pallas_call(
        gram_kernel,
        out_shape=jax.ShapeDtypeStruct((nc * chips * piece, T), jnp.float32),
        name="gram",
    )(local, probe_cols, own_weights, own_slices)

    swap = [(0, 1), (1, 0)]
    halves = packed.reshape(nc, chips * piece, T)
    mine = lax.dynamic_index_in_dim(halves, core, 0, keepdims=False)
    other = lax.dynamic_index_in_dim(halves, 1 - core, 0, keepdims=False)
    mine = mine + lax.ppermute(other, "c", swap)
    parts = lax.all_to_all(mine.reshape(chips, piece, T), CHIPS, 0, 0, tiled=True)
    owned = jnp.sum(parts, axis=0, keepdims=True)
    spread = jnp.broadcast_to(owned, (chips, piece, T))
    whole = lax.all_to_all(spread, CHIPS, 0, 0, tiled=True).reshape(chips * piece, T)
    partner = lax.ppermute(whole, "c", swap)
    low = jnp.where(core == 0, whole, partner)
    high = jnp.where(core == 0, partner, whole)
    packed = jnp.concatenate([low, high], axis=0)

    basis, cross = pl.pallas_call(
        functools.partial(iterate_kernel, scale),
        out_shape=(
            jax.ShapeDtypeStruct((K, channels), jnp.float32),
            jax.ShapeDtypeStruct((channels, NS), jnp.float32),
        ),
        scratch_shapes=[pltpu.VMEM((channels, channels), jnp.float32)],
        name="iterate",
    )(packed)
    amps = multiply(basis, local)
    amps = lax.all_to_all(jnp.broadcast_to(amps[None], (nx, K, width)), "x", 0, 0, tiled=True)
    amps = jnp.concatenate([amps[i] for i in range(nx)], axis=1)
    own_basis = lax.dynamic_slice_in_dim(basis, own * rows, rows, 1)
    cleaned = cube - multiply(own_basis, amps, TN)
    return (cleaned, lax.dynamic_slice_in_dim(cross, own * rows, rows, 0))


def solution(mesh):
    devices = mesh.devices.reshape(4, 4, 2, 4)
    pix = ("y", "z", "c")
    in_specs = (P("x", pix), P(None, pix), P(pix), P(pix), P(pix))
    out_specs = (P("x", pix), P("x", None))
    return jax.shard_map(body, mesh=Mesh(devices, ("y", "z", "c", "x")), in_specs=in_specs, out_specs=out_specs, check_vma=False)
```

time: 1490 us -> 170 us (0.11)
  blocking collectives: 693 us -> 62.6 us
  waiting for transfers between devices: 496 us -> 35.8 us
  other arithmetic: 213 us -> 5.09 us
  Pallas kernels: 0 us -> 39.2 us
  matrix products: 27.2 us -> 6.97 us
    psum x5 -> x0, blocking collectives: 631 us -> none  [broadcast(): return lax.psum(kept, axis)]
    all_gather x6 -> x0, waiting for transfers between devices: 267 us -> none  [prefix(): pieces = lax.all_gather(value, axis)]
    select_n x192 -> x1, other arithmetic: 177 us -> 0.21 us  [body(): low = jnp.where(core == 0, whole, partner)]
    reduce_scatter x6 -> x0, waiting for transfers between devices: 104 us -> none  [fold_freq(): return lax.psum_scatter(term, 'freq', scatter_dimension=0, tiled=True)]
    psum x1 -> x0, waiting for transfers between devices: 99 us -> none  [broadcast(): return lax.psum(kept, axis)]
    all_to_all x0 -> x2, blocking collectives: none -> 62.6 us  [the longest x1 34.3 us: body(): lax.all_to_all(mine.reshape(chips, piece, T), CHIPS, 0, 0, tiled=True)]
    all_gather x5 -> x0, blocking collectives: 61.8 us -> none  [gather_rows(): return lax.all_gather(term, 'freq', axis=0, tiled=True)]
    pallas_call x0 -> x2, Pallas kernels: none -> 39.2 us  [the longest x1 28.1 us: body(): pl.pallas_call(functools.partial(iterate_kernel, scale), out_shape=(jax.S...]
  transfers between devices with their start and end apart: 15 -> 4, of which waited for: 14 -> 4; matrix products, arithmetic and copies ran while one was open for 2% -> 3% of each run, Pallas kernels for 0% -> 0%
where the time goes in v1:
time: 170 us
  blocking collectives  62.6 us (37%)
  Pallas kernels  39.2 us (23%)
  waiting for transfers between devices  35.8 us (21%)
  local copies, waits for them, and re-layouts  11.7 us (7%)
  starting transfers between devices  7.82 us (5%)
  matrix products  6.97 us (4%)
  other arithmetic  5.09 us (3%)
    all_to_all x1, blocking collectives, body(): lax.all_to_all(mine.reshape(chips, piece, T), CHIPS, 0, 0, tiled=True)  34.3 us
    all_to_all x1, blocking collectives, body(): lax.all_to_all(spread, CHIPS, 0, 0, tiled=True).reshape(chips * piece, T)  28.3 us
    pallas_call x1, Pallas kernels, body(): pl.pallas_call(functools.partial(iterate_kernel, scale), out_shape=(jax.S...  28.1 us
    all_to_all x1, waiting for transfers between devices, body(): local = lax.all_to_all(cube, 'x', split_axis=1, concat_axis=0, tiled=True)  23 us
    pallas_call x1, Pallas kernels, body(): pl.pallas_call(gram_kernel, out_shape=jax.ShapeDtypeStruct((nc * chips *...  11.2 us
    dot_general x2, matrix products, multiply(): lax.dot_general(left, right, dims, precision=HIGHEST, preferred_element_t...  6.97 us
    all_to_all x1, waiting for transfers between devices, body(): lax.all_to_all(jnp.broadcast_to(amps[None], (nx, K, width)), 'x', 0, 0, t...  5.63 us
    all_to_all x1, starting transfers between devices, body(): local = lax.all_to_all(cube, 'x', split_axis=1, concat_axis=0, tiled=True)  4.4 us
  transfers between devices with their start and end apart: 4, of which 4 were waited for; matrix products, arithmetic and copies ran while one was open for 3% of the time, Pallas kernels for 0%

profile of v1, /device:TPU:0, one launch (start us, length us, event | category | flops | bytes accessed | tf_op | source)
XLA Modules:
  0.0 169.9 jit_solution(13820834686686577874)
XLA Ops:
  0.6 0.0 copy-start
  0.6 3.2 %copy.10 = f32[32,4,8,512]{3,2,0,1:T(8,128)} copy(f32[32,4,8,512]{3,2,1,0:T(8,128)} %bitcast.32) | data formatting | bytes 4194304 | tf_op jit(solution)/shard_map/all_to_all | solution.py:100
  3.8 4.4 %all-to-all-start = ((f32[256,4,512]{2,0,1:T(8,128)}), f32[256,4,512]{2,0,1:T(8,128)S(1)}, u32[]{:S(2)}, u32[]{:S(2)}) async-start(f32[256,4,512]{2,0,1:T(8,128)} %bitcast.33), calls=%async_computation | async-start | bytes 4194304 | tf_op jit(solution)/shard_map/all_to_all | solution.py:100
  8.2 1.3 dynamic-slice.7
  9.6 1.4 dynamic-slice_multiply_fusion
  10.9 0.0 copy-done
  10.9 0.6 constant_dynamic-slice_fusion.1.probes_ref
  11.6 23.0 %all-to-all-done = f32[256,4,512]{2,0,1:T(8,128)S(1)} async-done(((f32[256,4,512]{2,0,1:T(8,128)}), f32[256,4,512]{2,0,1:T(8,128)S(1)}, u32[]{:S(2)}, u32[]{:S(2)}) %all-to-all-start) | async-done | bytes 2097184 | tf_op jit(solution)/shard_map/all_to_all | solution.py:100
  34.6 0.0 copy-start.1
  34.6 1.3 copy-done.1
  35.9 11.2 %gram.1 = f32[6144,128]{1,0:T(8,128)} custom-call(f32[1024,512]{1,0:T(8,128)} %bitcast.28, f32[32,512]{1,0:T(8,128)} %constant_dynamic-slice_fusion.1.probes_ref, f32[1,512]{1,0:T(1,128)} %bitcast.37, s32[1,512]{1,0:T(1,128)} %bitcast.36), custom_call_target="tpu_custom_call" | custom-call | tf_op jit(solution)/shard_map/gram/pallas_call | solution.py:110
  47.0 0.0 copy-start.3
  47.0 2.8 %dynamic-slice_bitcast_fusion = f32[3072,128]{1,0:T(8,128)} fusion(f32[2,3072,128]{2,1,0:T(8,128)} %bitcast.30, s32[]{:T(128)S(6)} %select_n.31), kind=kLoop, calls=%fused_computation.4 | loop fusion | bytes 3145732 | tf_op jit(solution)/shard_map/jit(dynamic_index_in_dim)/squeeze | solution.py:119
  49.9 0.0 collective-permute-start
  49.9 3.7 %collective-permute-done = f32[3072,128]{1,0:T(8,128)} collective-permute-done((f32[3072,128]{1,0:T(8,128)}, f32[3072,128]{1,0:T(8,128)}, u32[]{:S(2)}, u32[]{:S(2)}) %collective-permute-start) | collective-permute-done | bytes 1572896 | tf_op jit(solution)/shard_map/ppermute | solution.py:120
  53.6 0.0 copy-done.3
  53.6 1.6 bitcast_add_fusion
  55.2 34.3 %all_to_all.34 = f32[64,48,128]{2,1,0:T(8,128)S(1)} all-to-all(f32[64,48,128]{2,1,0:T(8,128)S(1)} %bitcast.34), channel_id=1, replica_groups=mesh['y'=4,'z'=4,'c'=2,'x'=4] {'y','z','x'}, dimensions={0} | all-to-all | bytes 3145728 | tf_op jit(solution)/shard_map/all_to_all | solution.py:121
  89.5 0.1 reduce_sum.9
  89.6 0.1 broadcast_in_dim.4
  89.8 28.3 %all_to_all.35 = f32[64,48,128]{2,1,0:T(8,128)S(1)} all-to-all(f32[64,48,128]{2,1,0:T(8,128)S(1)} %broadcast_in_dim.4), channel_id=1, replica_groups=mesh['y'=4,'z'=4,'c'=2,'x'=4] {'y','z','x'}, dimensions={0} | all-to-all | bytes 3145728 | tf_op jit(solution)/shard_map/all_to_all | solution.py:124
  118.0 0.0 collective-permute-start.1
  118.0 3.4 %collective-permute-done.1 = f32[3072,128]{1,0:T(8,128)S(1)} collective-permute-done((f32[3072,128]{1,0:T(8,128)S(1)}, f32[3072,128]{1,0:T(8,128)S(1)}, u32[]{:S(2)}, u32[]{:S(2)}) %collective-permute-start.1) | collective-permute-done | bytes 1572896 | tf_op jit(solution)/shard_map/ppermute | solution.py:125
  121.4 0.2 broadcast_select_fusion.1
  121.6 1.8 %pad_maximum_fusion.packed_ref = f32[6144,128]{1,0:T(8,128)} fusion(f32[3072,128]{1,0:T(8,128)S(1)} %get-tuple-element.7, f32[3072,128]{1,0:T(8,128)S(1)} %get-tuple-element.6), kind=kLoop, calls=%fused_computation | loop fusion | flops 786432 | bytes 6291456 | tf_op jit(solution)/shard_map/concatenate | solution.py:128
  123.5 0.0 copy-start.2
  123.5 28.1 %iterate.1 = (f32[32,1024]{1,0:T(8,128)}, f32[1024,128]{1,0:T(8,128)}) custom-call(f32[6144,128]{1,0:T(8,128)} %pad_maximum_fusion.packed_ref), custom_call_target="tpu_custom_call" | custom-call | tf_op jit(solution)/shard_map/iterate/pallas_call | solution.py:130
  151.5 0.0 copy-done.2
  151.5 2.2 %fusion.10 = f32[32,512]{1,0:T(8,128)S(1)} fusion(f32[32,1024]{1,0:T(8,128)} %get-tuple-element.4, f32[1024,512]{1,0:T(8,128)S(1)} %bitcast.29), kind=kOutput, calls=%fused_computation.25 | convolution fusion | flops 201326592 | bytes 2293760 | tf_op jit(solution)/shard_map/dot_general | solution.py:22
  153.7 0.7 broadcast_in_dim.5
  154.5 3.4 %all-to-all-start.3 = ((f32[4,32,512]{2,1,0:T(8,128)}), f32[4,32,512]{2,1,0:T(8,128)S(1)}, u32[]{:S(2)}, u32[]{:S(2)}) async-start(f32[4,32,512]{2,1,0:T(8,128)} %broadcast_in_dim.5), calls=%async_computation.3 | async-start | bytes 524288 | tf_op jit(solution)/shard_map/all_to_all | solution.py:140
  157.9 1.6 constant_dynamic-slice_fusion
  159.5 5.6 %all-to-all-done.3 = f32[4,32,512]{2,1,0:T(8,128)S(1)} async-done(((f32[4,32,512]{2,1,0:T(8,128)}), f32[4,32,512]{2,1,0:T(8,128)S(1)}, u32[]{:S(2)}, u32[]{:S(2)}) %all-to-all-start.3) | async-done | bytes 262176 | tf_op jit(solution)/shard_map/all_to_all | solution.py:140
  165.1 4.8 %convolution_subtract_fusion = f32[256,2048]{1,0:T(8,128)} fusion(f32[256,2048]{1,0:T(8,128)} %param.5, f32[32,512]{1,0:T(8,128)S(1)} %get-tuple-element.9, f32[32,512]{1,0:T(8,128)S(1)} %get-tuple-element.10, f32[32,512]{1,0:T(8,128)S(1)} %get-tuple-element.11, f32[32,512]{1,0:T(8,128)S(1)} %get-tuple-element.8, f32[32,1024]{1,0:T(8,128)} %get-tuple-element.4, ...), kind=kOutput, calls=%fused_computation.1 | convolution fusion | flops 202047488 | bytes 4489220 | tf_op jit(solution)/shard_map/dot_general | solution.py:22
  (1 shorter events, 0.0 us)
Async XLA Ops:
  0.6 10.3 %copy-start = (f32[32,2048]{1,0:T(8,128)S(1)}, f32[32,2048]{1,0:T(8,128)}, u32[]{:S(2)}) copy-start(f32[32,2048]{1,0:T(8,128)} %param.6) | copy-start | bytes 786436
  3.8 30.7 %all-to-all-start = ((f32[256,4,512]{2,0,1:T(8,128)}), f32[256,4,512]{2,0,1:T(8,128)S(1)}, u32[]{:S(2)}, u32[]{:S(2)}) async-start(f32[256,4,512]{2,0,1:T(8,128)} %bitcast.33), calls=%async_computation | async-start | bytes 4194304 | tf_op jit(solution)/shard_map/all_to_all | solution.py:100
  34.6 1.3 copy-start.1
  47.0 6.6 %copy-start.3 = (f32[6144,128]{1,0:T(8,128)S(1)}, f32[6144,128]{1,0:T(8,128)}, u32[]{:S(2)}) copy-start(f32[6144,128]{1,0:T(8,128)} %gram.1) | copy-start | bytes 9437188
  49.9 3.8 %collective-permute-start = (f32[3072,128]{1,0:T(8,128)}, f32[3072,128]{1,0:T(8,128)}, u32[]{:S(2)}, u32[]{:S(2)}) collective-permute-start(f32[3072,128]{1,0:T(8,128)} %dynamic-slice_bitcast_fusion), channel_id=1, source_target_pairs={{0,4},{4,0},{1,5},{5,1},{2,6},{6,2},{3,7},{7,3},{8,12},{12,8},{9,1... | collective-permute-start | bytes 4718600 | tf_op jit(solution)/shard_map/ppermute | solution.py:120
  118.0 3.4 %collective-permute-start.1 = (f32[3072,128]{1,0:T(8,128)S(1)}, f32[3072,128]{1,0:T(8,128)S(1)}, u32[]{:S(2)}, u32[]{:S(2)}) collective-permute-start(f32[3072,128]{1,0:T(8,128)S(1)} %bitcast.35), channel_id=1, source_target_pairs={{0,4},{4,0},{1,5},{5,1},{2,6},{6,2},{3,7},{7,3},{8,12},{12,8},{9,1... | collective-permute-start | bytes 4718600 | tf_op jit(solution)/shard_map/ppermute | solution.py:125
  123.5 28.1 %copy-start.2 = (f32[256,4,512]{2,0,1:T(8,128)S(1)}, f32[256,4,512]{2,0,1:T(8,128)}, u32[]{:S(2)}) copy-start(f32[256,4,512]{2,0,1:T(8,128)} %copy-done.1) | copy-start | bytes 6291460
  154.5 10.6 %all-to-all-start.3 = ((f32[4,32,512]{2,1,0:T(8,128)}), f32[4,32,512]{2,1,0:T(8,128)S(1)}, u32[]{:S(2)}, u32[]{:S(2)}) async-start(f32[4,32,512]{2,1,0:T(8,128)} %broadcast_in_dim.5), calls=%async_computation.3 | async-start | bytes 524288 | tf_op jit(solution)/shard_map/all_to_all | solution.py:140

commit v2 on v0

v2 whole, which is shorter than its diff:
```python
import functools

import jax
import jax.numpy as jnp
from jax import lax
from jax.experimental import pallas as pl
from jax.experimental.pallas import tpu as pltpu
from jax.sharding import Mesh, PartitionSpec as P

NS = 128
ITERS = 4
K = 32
T = 128
NX = 4
CHIPS = ("y", "z", "x")
SWAP = [(0, 1), (1, 0)]
NN = (((1,), (0,)), ((), ()))
NT = (((1,), (1,)), ((), ()))
TN = (((0,), (0,)), ((), ()))
F32 = jnp.float32

NEXT = 0
SKIP = NEXT + NX * 2 * T
DIAG = SKIP + 2 * 2 * T
SIDE = DIAG + NX * T
SKETCH = SIDE + 2 * T
TABLE = SKETCH + NX * K
USED = TABLE + NX * T

VMEM = pl.BlockSpec(memory_space=pltpu.VMEM)
SMEM = pl.BlockSpec(memory_space=pltpu.SMEM)


def dot(left, right, dims=NN):
    return lax.dot_general(left, right, dims, preferred_element_type=F32)


def split(value):
    high = value.astype(jnp.bfloat16)
    rest = value - high.astype(F32)
    mid = rest.astype(jnp.bfloat16)
    return high, mid, (rest - mid.astype(F32)).astype(jnp.bfloat16)


def product(left, right, dims):
    rows = left[0].shape[0]
    one = dot(left[0], right[2], dims)
    two = dot(jnp.concatenate(left[:2], axis=0), right[1], dims)
    three = dot(jnp.concatenate(left, axis=0), right[0], dims)
    small = one + two[rows:] + three[2 * rows :]
    return small + (two[:rows] + three[rows : 2 * rows]) + three[:rows]


def gram_kernel(rels, new, pairs, first, meta_ref, aux_ref, aux_partner_ref, *refs):
    count = len(rels)
    pieces, rest = refs[: 2 * count], refs[2 * count :]
    if not first:
        rest[1][...] = rest[0][...]
        rest = rest[1:]
    out_ref, terms = rest
    own, core = meta_ref[0], meta_ref[1]
    for index in range(count):
        for side in range(2):
            for term, value in enumerate(split(pieces[2 * index + side][...])):
                width = value.shape[1]
                terms[index, term, :, side * width : (side + 1) * width] = value

    def whole(index):
        return tuple(terms[index, term] for term in range(3))

    def half(index):
        return tuple(terms[index, term, pl.ds(pl.multiple_of(core * T, T), T), :] for term in range(3))

    def store(base, at, value):
        size = value.shape[0]
        out_ref[pl.ds(pl.multiple_of(base + at * size, size), size), :] = value

    aux = jnp.concatenate([aux_ref[...], aux_partner_ref[...]], axis=1)
    probes = split(aux[:K])
    levels = lax.broadcasted_iota(jnp.int32, (NS, aux.shape[1]), 0).astype(F32)
    table = split(jnp.where(levels == aux[K + 1 : K + 2], aux[K : K + 1], 0.0))
    for rel in new:
        index = rels.index(rel)
        block = lax.rem(own - rel + NX, NX)
        mine = half(index)
        square = product(mine, whole(index), NT)
        left, right = square[:, :T], square[:, T:]
        store(DIAG, block, jnp.where(core == 0, left, right))

        @pl.when((block < 2) == (core == 0))
        def _():
            store(SIDE, lax.rem(block, 2), jnp.where(core == 0, right, left))

        store(TABLE, block, product(mine, table, NT))
        store(SKETCH, block, product(probes, mine, NT))
    for rows, columns, near in pairs:
        low, high = rels.index(rows), rels.index(columns)
        block = lax.rem(own - rows + NX, NX)
        if near:
            result = product(half(low), whole(high), NT)
            base = NEXT
        else:
            flip = block >= 2
            block = lax.rem(block, 2)
            low, high = jnp.where(flip, high, low), jnp.where(flip, low, high)
            result = product(half(low), whole(high), NT)
            base = SKIP
        size = result.shape[0]
        at = pl.multiple_of(base + block * 2 * size, 2 * size)
        out_ref[pl.ds(at, size), :] = result[:, :T]
        out_ref[pl.ds(at + size, size), :] = result[:, T:]
    if first and USED < out_ref.shape[0]:
        out_ref[USED:, :] = jnp.zeros((out_ref.shape[0] - USED, T), F32)


def inverse_factor(gram, panel=16):
    rows = lax.broadcasted_iota(jnp.int32, (K, T), 0)
    lanes = lax.broadcasted_iota(jnp.int32, (K, T), 1)
    unit = jnp.where(lanes == rows + K, 1.0, 0.0).astype(F32)
    wide = jnp.concatenate([gram, jnp.zeros((K, T - K), F32)], axis=1) + unit
    for base in range(0, K, panel):
        columns = [jnp.broadcast_to(wide[:, base + j : base + j + 1], (K, T)) for j in range(panel)]
        for j in range(panel):
            k = base + j
            if k == K - 1:
                break
            inverse = 1.0 / columns[j][k : k + 1, :]
            below = jnp.where(rows > k, columns[j], 0.0)
            scaled = wide[k : k + 1, :] * inverse
            heads = [columns[i][k : k + 1, :] * inverse for i in range(j + 1, panel)]
            wide = wide - below * scaled
            for head, i in zip(heads, range(j + 1, panel)):
                columns[i] = columns[i] - below * head
    pivots = jnp.sum(jnp.where(lanes == rows, wide, 0.0), axis=1, keepdims=True)
    return wide[:, K : 2 * K] * lax.rsqrt(pivots)


def gram_of(terms):
    stacked = jnp.concatenate(terms, axis=0)
    all_pairs = dot(stacked, stacked, NT)

    def part(i, j):
        return all_pairs[i * K : (i + 1) * K, j * K : (j + 1) * K]

    return (part(0, 2) + part(2, 0) + part(1, 1)) + (part(0, 1) + part(1, 0)) + part(0, 0)


def deep(terms, order, axis):
    return jnp.concatenate([terms[i] for i in order], axis=axis)


LEFT = (2, 1, 0, 1, 0, 0)
RIGHT = (0, 1, 2, 0, 1, 0)


def iterate_kernel(scale, meta_ref, mine_ref, partner_ref, r0, r1, r2, r3, amps_ref, own_basis_ref, cross_ref, full, basis_ref, sums_ref):
    own, core = meta_ref[0], meta_ref[1]
    locals_ = (r0, r1, r2, r3)

    def load(side, at, size):
        same = mine_ref[at : at + size, :]
        other = partner_ref[at : at + size, :]
        return jnp.where(core == side, same, other)

    def place(row, column, value):
        for term, part in enumerate(split(value)):
            full[term, row : row + value.shape[0], column : column + value.shape[1]] = part

    step = 2 * T
    factor = jnp.concatenate([load(side, SKETCH + a * K, K) for a in range(NX) for side in range(2)], axis=1)
    for side in range(2):
        for a in range(NX):
            row = a * step + side * T
            place(row, row, load(side, DIAG + a * T, T))
            sums_ref[row : row + T, :] = load(side, TABLE + a * T, T)
            if (a < 2) == (side == 0):
                value = load(side, SIDE + (a % 2) * T, T)
                column = a * step + (1 - side) * T
                place(row, column, value)
                place(column, row, value.T)
            spans = [(NEXT + a * step, (a + 1) % NX)]
            if a < 2:
                spans.append((SKIP + a * step, a + 2))
            for at, b in spans:
                for part in range(2):
                    value = load(side, at + part * T, T)
                    column = b * step + part * T
                    place(row, column, value)
                    place(column, row, value.T)
    for iteration in range(ITERS + 1):
        terms = split(factor)
        inverse = inverse_factor(gram_of(terms))
        ahead = factor
        if iteration < ITERS:
            ahead = product(terms, (full[0], full[1], full[2]), NN)
        factor = dot(deep(split(inverse), LEFT, 1), deep(split(ahead), RIGHT, 0))
    basis_ref[...] = factor
    amps = jnp.zeros(amps_ref.shape, F32)
    for rel in range(NX):
        block = lax.rem(own - rel + NX, NX)
        rows = basis_ref[:, pl.ds(pl.multiple_of(block * step, step), step)]
        amps = amps + product(split(rows), split(locals_[rel][...]), NN)
    amps_ref[...] = amps
    at = pl.multiple_of(own * step, step)
    own_basis = basis_ref[:, pl.ds(at, step)]
    own_basis_ref[...] = own_basis
    inner = product(split(factor), split(sums_ref[...]), NN)
    fitted = dot(deep(split(own_basis), LEFT, 0), deep(split(inner), RIGHT, 0), TN)
    cross_ref[...] = (sums_ref[pl.ds(at, step), :] - fitted) * scale


def clean_kernel(meta_ref, basis_ref, a0, a1, a2, a3, cube_ref, out_ref):
    rel = lax.rem(meta_ref[0] - pl.program_id(0) + NX, NX)
    amps = jnp.where(rel < 2, jnp.where(rel == 0, a0[...], a1[...]), jnp.where(rel == 2, a2[...], a3[...]))
    fitted = dot(deep(split(basis_ref[...]), LEFT, 0), deep(split(amps), RIGHT, 0), TN)
    out_ref[...] = cube_ref[...] - fitted


def body(cube, probes, galaxy, slices, valid):
    chips = lax.axis_size(CHIPS)
    rows, columns = cube.shape
    pixels = chips // NX * 2 * columns
    scale = (float(pixels) / float(NS)) ** (-0.5)
    own, core = lax.axis_index("x"), lax.axis_index("c")
    meta = jnp.stack([own, core]).astype(jnp.int32)
    width = columns // NX

    def shift(value, by):
        return lax.ppermute(value, "x", [(i, (i + by) % NX) for i in range(NX)])

    def columns_of(value, block):
        return lax.dynamic_slice_in_dim(value, block * width, width, 1)

    received = [columns_of(cube, own)]
    for by in range(1, NX):
        received.append(shift(columns_of(cube, lax.rem(own + by, NX)), by))
    partner = [lax.ppermute(piece, "c", SWAP) for piece in received]
    weights = galaxy * valid.astype(F32)
    extra = jnp.zeros((8, columns), F32).at[0].set(weights).at[1].set(slices.astype(F32))
    aux = columns_of(jnp.concatenate([probes, extra], axis=0), own)
    aux_partner = lax.ppermute(aux, "c", SWAP)

    piece = -(-USED // (chips * 8)) * 8
    shape = jax.ShapeDtypeStruct((chips * piece, T), F32)

    def gram(rels, new, pairs, packed):
        first = packed is None
        blocks = [value for rel in rels for value in (received[rel], partner[rel])]
        args = [meta, aux, aux_partner] + blocks + ([] if first else [packed])
        return pl.pallas_call(
            functools.partial(gram_kernel, rels, new, pairs, first),
            out_shape=shape,
            in_specs=[SMEM] + [VMEM] * (len(args) - 1),
            out_specs=VMEM,
            scratch_shapes=[pltpu.VMEM((len(rels), 3, rows, 2 * width), jnp.bfloat16)],
            name="gram",
        )(*args)

    packed = gram((0, 1), (0, 1), ((1, 0, True),), None)
    packed = gram((0, 1, 3), (3,), ((0, 3, True), (1, 3, False)), packed)
    packed = gram((0, 1, 3, 2), (2,), ((2, 1, True), (3, 2, True), (0, 2, False)), packed)

    parts = lax.all_to_all(packed.reshape(chips, piece, T), CHIPS, 0, 0, tiled=True)
    owned = jnp.sum(parts, axis=0, keepdims=True)
    spread = jnp.broadcast_to(owned, (chips, piece, T))
    mine = lax.all_to_all(spread, CHIPS, 0, 0, tiled=True).reshape(chips * piece, T)
    other = lax.ppermute(mine, "c", SWAP)

    channels = rows * NX
    amps, own_basis, cross = pl.pallas_call(
        functools.partial(iterate_kernel, scale),
        out_shape=(
            jax.ShapeDtypeStruct((K, width), F32),
            jax.ShapeDtypeStruct((K, rows), F32),
            jax.ShapeDtypeStruct((rows, NS), F32),
        ),
        in_specs=[SMEM] + [VMEM] * 6,
        out_specs=(VMEM, VMEM, VMEM),
        scratch_shapes=[
            pltpu.VMEM((3, channels, channels), jnp.bfloat16),
            pltpu.VMEM((K, channels), F32),
            pltpu.VMEM((channels, NS), F32),
        ],
        name="iterate",
    )(meta, mine, other, *received)
    spread_amps = [amps] + [shift(amps, by) for by in range(1, NX)]
    block = pl.BlockSpec((rows, width), lambda j: (0, j))
    cleaned = pl.pallas_call(
        clean_kernel,
        grid=(NX,),
        out_shape=jax.ShapeDtypeStruct(cube.shape, F32),
        in_specs=[SMEM] + [VMEM] * 5 + [block],
        out_specs=block,
        name="clean",
    )(meta, own_basis, *spread_amps, cube)
    return (cleaned, cross)


def solution(mesh):
    devices = mesh.devices.reshape(4, 4, 2, NX)
    pix = ("y", "z", "c")
    in_specs = (P("x", pix), P(None, pix), P(pix), P(pix), P(pix))
    out_specs = (P("x", pix), P("x", None))
    return jax.shard_map(body, mesh=Mesh(devices, ("y", "z", "c", "x")), in_specs=in_specs, out_specs=out_specs, check_vma=False)
```

time: 1490 us -> 155 us (0.10)
  blocking collectives: 693 us -> 64 us
  waiting for transfers between devices: 496 us -> 31.8 us
  other arithmetic: 213 us -> 0.79 us
  Pallas kernels: 0 us -> 42.9 us
  matrix products: 27.2 us -> 0 us
  local copies, waits for them, and re-layouts: 25.4 us -> 6.33 us
    psum x5 -> x0, blocking collectives: 631 us -> none  [broadcast(): return lax.psum(kept, axis)]
    all_gather x6 -> x0, waiting for transfers between devices: 267 us -> none  [prefix(): pieces = lax.all_gather(value, axis)]
    select_n x192 -> x0, other arithmetic: 177 us -> none  [the longest x186 176 us: lap(): return jnp.where(position < mine, longer, total)]
    reduce_scatter x6 -> x0, waiting for transfers between devices: 104 us -> none  [fold_freq(): return lax.psum_scatter(term, 'freq', scatter_dimension=0, tiled=True)]
    psum x1 -> x0, waiting for transfers between devices: 99 us -> none  [broadcast(): return lax.psum(kept, axis)]
    all_to_all x0 -> x2, blocking collectives: none -> 64 us  [the longest x1 35.7 us: body(): lax.all_to_all(packed.reshape(chips, piece, T), CHIPS, 0, 0, tiled=True)]
    all_gather x5 -> x0, blocking collectives: 61.8 us -> none  [gather_rows(): return lax.all_gather(term, 'freq', axis=0, tiled=True)]
    pallas_call x0 -> x5, Pallas kernels: none -> 42.9 us  [the longest x3 25.9 us: gram(): pl.pallas_call(functools.partial(gram_kernel, rels, new, pairs, first), o...]
  transfers between devices with their start and end apart: 15 -> 12, of which waited for: 14 -> 8; matrix products, arithmetic and copies ran while one was open for 2% -> 1% of each run, Pallas kernels for 0% -> 11%
where the time goes in v2:
time: 155 us
  blocking collectives  64 us (41%)
  Pallas kernels  42.9 us (28%)
  waiting for transfers between devices  31.8 us (21%)
  starting transfers between devices  8.48 us (5%)
  local copies, waits for them, and re-layouts  6.33 us (4%)
    all_to_all x1, blocking collectives, body(): lax.all_to_all(packed.reshape(chips, piece, T), CHIPS, 0, 0, tiled=True)  35.7 us
    all_to_all x1, blocking collectives, body(): lax.all_to_all(spread, CHIPS, 0, 0, tiled=True).reshape(chips * piece, T)  28.3 us
    ppermute x6, waiting for transfers between devices, shift(): return lax.ppermute(value, 'x', [(i, (i + by) % NX) for i in range(NX)])  27.7 us
    pallas_call x3, Pallas kernels, gram(): pl.pallas_call(functools.partial(gram_kernel, rels, new, pairs, first), o...  25.9 us
    pallas_call x1, Pallas kernels, body(): pl.pallas_call(functools.partial(iterate_kernel, scale), out_shape=(jax.S...  12.7 us
    ppermute x6, starting transfers between devices, shift(): return lax.ppermute(value, 'x', [(i, (i + by) % NX) for i in range(NX)])  7.9 us
    pallas_call x1, Pallas kernels, body(): pl.pallas_call(clean_kernel, grid=(NX,), out_shape=jax.ShapeDtypeStruct(c...  4.28 us
    unnamed x34, local copies, waits for them, and re-layouts  4.24 us
  transfers between devices with their start and end apart: 12, of which 8 were waited for; matrix products, arithmetic and copies ran while one was open for 1% of the time, Pallas kernels for 11%

profile of v2, /device:TPU:0, one launch (start us, length us, event | category | flops | bytes accessed | tf_op | source)
XLA Modules:
  0.0 155.1 jit_solution(15238978886725163981)
XLA Ops:
  0.7 0.0 copy-start.16
  0.7 0.0 copy-start.14
  0.7 1.8 %constant_dynamic-slice_fusion = (f32[256,512]{1,0:T(8,128)S(1)}, f32[256,512]{1,0:T(8,128)S(1)}, f32[256,512]{1,0:T(8,128)S(1)}, f32[256,512]{1,0:T(8,128)S(1)}) fusion(f32[256,2048]{1,0:T(8,128)} %cube_ref.1, s32[]{:T(128)S(6)} %select_n.16, s32[]{:T(128)S(6)} %select_n.15, s32[]{:T(128)S(6)} %select_n.14, s32[]{:T(128)S(6)} %select_n.13), kind=kLoop, calls=%fused_computation.4 | loop fusion | bytes 4194320 | tf_op jit(solution)/shard_map/dynamic_slice | solution.py:232
  2.5 0.0 copy-start
  2.5 1.7 %collective-permute-start.2 = (f32[256,512]{1,0:T(8,128)S(1)}, f32[256,512]{1,0:T(8,128)S(1)}, u32[]{:S(2)}, u32[]{:S(2)}) collective-permute-start(f32[256,512]{1,0:T(8,128)S(1)} %get-tuple-element.34), channel_id=1, source_target_pairs={{0,1},{1,2},{2,3},{3,0},{4,5},{5,6},{6,7},{7,4},{8,9},{9,10},{10,1... | collective-permute-start | bytes 1572872 | tf_op jit(solution)/shard_map/ppermute | solution.py:229
  4.1 1.6 %collective-permute-start.4 = (f32[256,512]{1,0:T(8,128)S(1)}, f32[256,512]{1,0:T(8,128)S(1)}, u32[]{:S(2)}, u32[]{:S(2)}) collective-permute-start(f32[256,512]{1,0:T(8,128)S(1)} %get-tuple-element.33), channel_id=1, source_target_pairs={{0,3},{1,0},{2,1},{3,2},{4,7},{5,4},{6,5},{7,6},{8,11},{9,8},{10,9... | collective-permute-start | bytes 1572872 | tf_op jit(solution)/shard_map/ppermute | solution.py:229
  5.8 1.9 %collective-permute-start.6 = (f32[256,512]{1,0:T(8,128)S(1)}, f32[256,512]{1,0:T(8,128)}, u32[]{:S(2)}, u32[]{:S(2)}) collective-permute-start(f32[256,512]{1,0:T(8,128)S(1)} %get-tuple-element.32), channel_id=1, source_target_pairs={{0,2},{1,3},{2,0},{3,1},{4,6},{5,7},{6,4},{7,5},{8,10},{9,11},{10,... | collective-permute-start | bytes 1572872 | tf_op jit(solution)/shard_map/ppermute | solution.py:229
  7.7 0.0 collective-permute-start.1
  7.7 9.6 %collective-permute-done.2.refs_2_.r1 = f32[256,512]{1,0:T(8,128)S(1)} collective-permute-done((f32[256,512]{1,0:T(8,128)S(1)}, f32[256,512]{1,0:T(8,128)S(1)}, u32[]{:S(2)}, u32[]{:S(2)}) %collective-permute-start.2) | collective-permute-done | bytes 524320 | tf_op jit(solution)/shard_map/ppermute | solution.py:229
  17.3 0.0 collective-permute-start.3
  17.3 1.6 %collective-permute-done.4.refs_4_.r3 = f32[256,512]{1,0:T(8,128)S(1)} collective-permute-done((f32[256,512]{1,0:T(8,128)S(1)}, f32[256,512]{1,0:T(8,128)S(1)}, u32[]{:S(2)}, u32[]{:S(2)}) %collective-permute-start.4) | collective-permute-done | bytes 524320 | tf_op jit(solution)/shard_map/ppermute | solution.py:229
  18.9 0.0 collective-permute-start.5
  18.9 10.9 %collective-permute-done.6.refs_6_.r2 = f32[256,512]{1,0:T(8,128)} collective-permute-done((f32[256,512]{1,0:T(8,128)S(1)}, f32[256,512]{1,0:T(8,128)}, u32[]{:S(2)}, u32[]{:S(2)}) %collective-permute-start.6) | collective-permute-done | bytes 524320 | tf_op jit(solution)/shard_map/ppermute | solution.py:229
  29.9 0.0 collective-permute-start.7
  29.9 0.0 copy-done.16
  29.9 0.2 scatter.9
  30.1 0.0 copy-done.10
  30.2 0.0 copy-start.8
  30.2 0.6 collective-permute-start
  30.7 0.6 pad_add_fusion.meta_ref
  31.4 0.7 collective-permute-done.aux_partner_ref
  32.1 0.0 collective-permute-done.1.refs_1_
  32.1 0.0 collective-permute-done.3.refs_3_
  32.2 0.6 copy-done.9
  32.8 0.2 copy-done.3
  33.0 0.8 copy-done.4
  33.7 8.2 %gram.3.refs_6_ = f32[3072,128]{1,0:T(8,128)} custom-call(s32[2]{0:T(128)} %pad_add_fusion.meta_ref, f32[40,512]{1,0:T(8,128)} %copy-done.8, f32[40,512]{1,0:T(8,128)} %copy-done.9, f32[256,512]{1,0:T(8,128)} %copy-done, f32[256,512]{1,0:T(8,128)} %copy-done.3, f32[256,512]{1,0:T(8,128)} %copy-done.1, f32[256,512]{1,0:T(8,128)} %copy-done.4), custom_call_target="tpu_custom_call" | custom-call | tf_op jit(solution)/shard_map/gram/pallas_call | solution.py:250
  41.9 0.0 collective-permute-done.5.refs_5_
  41.9 0.8 copy-done.6
  42.7 8.6 %gram.4.refs_8_ = f32[3072,128]{1,0:T(8,128)} custom-call(s32[2]{0:T(128)} %pad_add_fusion.meta_ref, f32[40,512]{1,0:T(8,128)} %copy-done.8, f32[40,512]{1,0:T(8,128)} %copy-done.9, f32[256,512]{1,0:T(8,128)} %copy-done, f32[256,512]{1,0:T(8,128)} %copy-done.3, f32[256,512]{1,0:T(8,128)} %copy-done.1, f32[256,512]{1,0:T(8,128)} %copy-done.4, ...), custom_call_target="tpu_custom_call" | custom-call | tf_op jit(solution)/shard_map/gram/pallas_call | solution.py:250
  51.3 0.0 collective-permute-done.7.refs_7_
  51.3 9.1 %gram.5 = f32[3072,128]{1,0:T(8,128)} custom-call(s32[2]{0:T(128)} %pad_add_fusion.meta_ref, f32[40,512]{1,0:T(8,128)} %copy-done.8, f32[40,512]{1,0:T(8,128)} %copy-done.9, f32[256,512]{1,0:T(8,128)} %copy-done, f32[256,512]{1,0:T(8,128)} %copy-done.3, f32[256,512]{1,0:T(8,128)} %copy-done.1, f32[256,512]{1,0:T(8,128)} %copy-done.4, f32[256,512]{1,0:T(8,128)} %copy-done.5, ...), custom_call_target="tpu_custom_call" | custom-call | tf_op jit(solution)/shard_map/gram/pallas_call | solution.py:250
  60.5 35.7 %all_to_all.10 = f32[64,48,128]{2,1,0:T(8,128)S(1)} all-to-all(f32[64,48,128]{2,1,0:T(8,128)} %bitcast.8), channel_id=1, replica_groups=mesh['y'=4,'z'=4,'c'=2,'x'=4] {'y','z','x'}, dimensions={0} | all-to-all | bytes 3145728 | tf_op jit(solution)/shard_map/all_to_all | solution.py:263
  96.2 0.1 reduce_sum.9
  96.3 0.1 broadcast_in_dim.2
  96.4 28.3 %all_to_all.11 = f32[64,48,128]{2,1,0:T(8,128)S(1)} all-to-all(f32[64,48,128]{2,1,0:T(8,128)S(1)} %broadcast_in_dim.2), channel_id=1, replica_groups=mesh['y'=4,'z'=4,'c'=2,'x'=4] {'y','z','x'}, dimensions={0} | all-to-all | bytes 3145728 | tf_op jit(solution)/shard_map/all_to_all | solution.py:266
  124.7 0.0 collective-permute-start.8
  124.7 3.4 %collective-permute-done.8.partner_ref = f32[3072,128]{1,0:T(8,128)S(1)} collective-permute-done((f32[3072,128]{1,0:T(8,128)S(1)}, f32[3072,128]{1,0:T(8,128)S(1)}, u32[]{:S(2)}, u32[]{:S(2)}) %collective-permute-start.8) | collective-permute-done | bytes 1572896 | tf_op jit(solution)/shard_map/ppermute | solution.py:267
  128.1 1.2 copy-done.7
  129.3 12.7 %iterate.1 = (f32[32,512]{1,0:T(8,128)}, f32[32,256]{1,0:T(8,128)}, f32[256,128]{1,0:T(8,128)}) custom-call(s32[2]{0:T(128)} %pad_add_fusion.meta_ref, f32[3072,128]{1,0:T(8,128)} %bitcast.7, f32[3072,128]{1,0:T(8,128)} %copy-done.7, f32[256,512]{1,0:T(8,128)} %copy-done, f32[256,512]{1,0:T(8,128)} %copy-done.1, ...), custom_call_target="tpu_custom_call" | custom-call | tf_op jit(solution)/shard_map/iterate/pallas_call | solution.py:270
  142.0 0.8 collective-permute-start.11
  142.8 1.7 %collective-permute-start.10 = (f32[32,512]{1,0:T(8,128)}, f32[32,512]{1,0:T(8,128)S(1)}, u32[]{:S(2)}, u32[]{:S(2)}) collective-permute-start(f32[32,512]{1,0:T(8,128)} %get-tuple-element.30.a0), channel_id=1, source_target_pairs={{0,2},{1,3},{2,0},{3,1},{4,6},{5,7},{6,4},{7,5},{8,10},{9,11},{10,... | collective-permute-start | bytes 196616 | tf_op jit(solution)/shard_map/ppermute | solution.py:229
  144.5 0.2 collective-permute-start.9
  144.6 2.4 %collective-permute-done.11.a3 = f32[32,512]{1,0:T(8,128)S(1)} collective-permute-done((f32[32,512]{1,0:T(8,128)}, f32[32,512]{1,0:T(8,128)S(1)}, u32[]{:S(2)}, u32[]{:S(2)}) %collective-permute-start.11) | collective-permute-done | bytes 65568 | tf_op jit(solution)/shard_map/ppermute | solution.py:229
  147.0 1.9 %collective-permute-done.10.a2 = f32[32,512]{1,0:T(8,128)S(1)} collective-permute-done((f32[32,512]{1,0:T(8,128)}, f32[32,512]{1,0:T(8,128)S(1)}, u32[]{:S(2)}, u32[]{:S(2)}) %collective-permute-start.10) | collective-permute-done | bytes 65568 | tf_op jit(solution)/shard_map/ppermute | solution.py:229
  149.0 1.2 collective-permute-done.9.a1
  150.2 0.6 copy-done.13
  150.8 4.3 %clean.1 = f32[256,2048]{1,0:T(8,128)} custom-call(s32[2]{0:T(128)} %pad_add_fusion.meta_ref, f32[32,256]{1,0:T(8,128)} %get-tuple-element.29.basis_ref, f32[32,512]{1,0:T(8,128)} %get-tuple-element.30.a0, f32[32,512]{1,0:T(8,128)} %copy-done.13, f32[32,512]{1,0:T(8,128)} %copy-done.12, f32[32,512]{1,0:T(8,128)} %copy-done.11, f32[256,2048]{1,0:T(8,128)} %cube_ref.1), custom_call_target="tpu_custom_call" | custom-call | tf_op jit(solution)/shard_map/clean/pallas_call | solution.py:288
  (26 shorter events, 0.1 us)
Async XLA Ops:
  0.7 29.2 %copy-start.16 = (s32[2048]{0:T(1024)S(1)}, s32[2048]{0:T(1024)}, u32[]{:S(2)}) copy-start(s32[2048]{0:T(1024)} %param.12) | copy-start | bytes 24580
  0.7 29.2 %copy-start.14 = (f32[2048]{0:T(1024)S(1)}, f32[2048]{0:T(1024)}, u32[]{:S(2)}) copy-start(f32[2048]{0:T(1024)} %param.11) | copy-start | bytes 24580
  0.7 29.2 %copy-start.15 = (s32[2048]{0:T(1024)S(1)}, s32[2048]{0:T(1024)}, u32[]{:S(2)}) copy-start(s32[2048]{0:T(1024)} %param.13) | copy-start | bytes 24580
  0.7 29.4 %copy-start.10 = (f32[32,2048]{1,0:T(8,128)S(1)}, f32[32,2048]{1,0:T(8,128)}, u32[]{:S(2)}) copy-start(f32[32,2048]{1,0:T(8,128)} %param.10) | copy-start | bytes 786436
  2.5 29.7 %copy-start = (f32[256,512]{1,0:T(8,128)}, f32[256,512]{1,0:T(8,128)S(1)}, u32[]{:S(2)}) copy-start(f32[256,512]{1,0:T(8,128)S(1)} %get-tuple-element.35.refs_0_.r0) | copy-start | bytes 1572868
  2.5 14.9 %collective-permute-start.2 = (f32[256,512]{1,0:T(8,128)S(1)}, f32[256,512]{1,0:T(8,128)S(1)}, u32[]{:S(2)}, u32[]{:S(2)}) collective-permute-start(f32[256,512]{1,0:T(8,128)S(1)} %get-tuple-element.34), channel_id=1, source_target_pairs={{0,1},{1,2},{2,3},{3,0},{4,5},{5,6},{6,7},{7,4},{8,9},{9,10},{10,1... | collective-permute-start | bytes 1572872 | tf_op jit(solution)/shard_map/ppermute | solution.py:229
  4.1 14.8 %collective-permute-start.4 = (f32[256,512]{1,0:T(8,128)S(1)}, f32[256,512]{1,0:T(8,128)S(1)}, u32[]{:S(2)}, u32[]{:S(2)}) collective-permute-start(f32[256,512]{1,0:T(8,128)S(1)} %get-tuple-element.33), channel_id=1, source_target_pairs={{0,3},{1,0},{2,1},{3,2},{4,7},{5,4},{6,5},{7,6},{8,11},{9,8},{10,9... | collective-permute-start | bytes 1572872 | tf_op jit(solution)/shard_map/ppermute | solution.py:229
  5.8 24.1 %collective-permute-start.6 = (f32[256,512]{1,0:T(8,128)S(1)}, f32[256,512]{1,0:T(8,128)}, u32[]{:S(2)}, u32[]{:S(2)}) collective-permute-start(f32[256,512]{1,0:T(8,128)S(1)} %get-tuple-element.32), channel_id=1, source_target_pairs={{0,2},{1,3},{2,0},{3,1},{4,6},{5,7},{6,4},{7,5},{8,10},{9,11},{10,... | collective-permute-start | bytes 1572872 | tf_op jit(solution)/shard_map/ppermute | solution.py:229
  7.7 24.4 %collective-permute-start.1 = (f32[256,512]{1,0:T(8,128)S(1)}, f32[256,512]{1,0:T(8,128)S(1)}, u32[]{:S(2)}, u32[]{:S(2)}) collective-permute-start(f32[256,512]{1,0:T(8,128)S(1)} %get-tuple-element.35.refs_0_.r0), channel_id=1, source_target_pairs={{0,4},{4,0},{1,5},{5,1},{2,6},{6,2},{3,7},{7,3},{8,12},{12,8},{9,1... | collective-permute-start | bytes 1572872 | tf_op jit(solution)/shard_map/ppermute | solution.py:237
  17.3 14.8 %copy-start.1 = (f32[256,512]{1,0:T(8,128)}, f32[256,512]{1,0:T(8,128)S(1)}, u32[]{:S(2)}) copy-start(f32[256,512]{1,0:T(8,128)S(1)} %collective-permute-done.2.refs_2_.r1) | copy-start | bytes 1572868
  17.3 14.8 %collective-permute-start.3 = (f32[256,512]{1,0:T(8,128)S(1)}, f32[256,512]{1,0:T(8,128)S(1)}, u32[]{:S(2)}, u32[]{:S(2)}) collective-permute-start(f32[256,512]{1,0:T(8,128)S(1)} %collective-permute-done.2.refs_2_.r1), channel_id=1, source_target_pairs={{0,4},{4,0},{1,5},{5,1},{2,6},{6,2},{3,7},{7,3},{8,12},{12,8},{9,1... | collective-permute-start | bytes 1572872 | tf_op jit(solution)/shard_map/ppermute | solution.py:237
  18.9 23.0 %copy-start.5 = (f32[256,512]{1,0:T(8,128)}, f32[256,512]{1,0:T(8,128)S(1)}, u32[]{:S(2)}) copy-start(f32[256,512]{1,0:T(8,128)S(1)} %collective-permute-done.4.refs_4_.r3) | copy-start | bytes 1572868
  18.9 23.0 %collective-permute-start.5 = (f32[256,512]{1,0:T(8,128)S(1)}, f32[256,512]{1,0:T(8,128)S(1)}, u32[]{:S(2)}, u32[]{:S(2)}) collective-permute-start(f32[256,512]{1,0:T(8,128)S(1)} %collective-permute-done.4.refs_4_.r3), channel_id=1, source_target_pairs={{0,4},{4,0},{1,5},{5,1},{2,6},{6,2},{3,7},{7,3},{8,12},{12,8},{9,1... | collective-permute-start | bytes 1572872 | tf_op jit(solution)/shard_map/ppermute | solution.py:237
  29.9 21.5 %collective-permute-start.7 = (f32[256,512]{1,0:T(8,128)}, f32[256,512]{1,0:T(8,128)}, u32[]{:S(2)}, u32[]{:S(2)}) collective-permute-start(f32[256,512]{1,0:T(8,128)} %collective-permute-done.6.refs_6_.r2), channel_id=1, source_target_pairs={{0,4},{4,0},{1,5},{5,1},{2,6},{6,2},{3,7},{7,3},{8,12},{12,8},{9,1... | collective-permute-start | bytes 1572872 | tf_op jit(solution)/shard_map/ppermute | solution.py:237
  30.2 2.0 %copy-start.8 = (f32[40,512]{1,0:T(8,128)}, f32[40,512]{1,0:T(8,128)S(1)}, u32[]{:S(2)}) copy-start(f32[40,512]{1,0:T(8,128)S(1)} %fusion.aux_ref) | copy-start | bytes 245764
  30.2 1.9 %collective-permute-start = (f32[40,512]{1,0:T(8,128)S(1)}, f32[40,512]{1,0:T(8,128)S(1)}, u32[]{:S(2)}, u32[]{:S(2)}) collective-permute-start(f32[40,512]{1,0:T(8,128)S(1)} %fusion.aux_ref), channel_id=1, source_target_pairs={{0,4},{4,0},{1,5},{5,1},{2,6},{6,2},{3,7},{7,3},{8,12},{12,8},{9,1... | collective-permute-start | bytes 245768 | tf_op jit(solution)/shard_map/ppermute | solution.py:241
  32.1 0.6 copy-start.9
  32.1 0.8 copy-start.3
  33.0 0.8 copy-start.4
  41.9 0.8 copy-start.6
  124.7 3.4 %copy-start.2 = (f32[64,48,128]{2,1,0:T(8,128)}, f32[64,48,128]{2,1,0:T(8,128)S(1)}, u32[]{:S(2)}) copy-start(f32[64,48,128]{2,1,0:T(8,128)S(1)} %all_to_all.11) | copy-start | bytes 4718596
  124.7 3.4 %collective-permute-start.8 = (f32[3072,128]{1,0:T(8,128)S(1)}, f32[3072,128]{1,0:T(8,128)S(1)}, u32[]{:S(2)}, u32[]{:S(2)}) collective-permute-start(f32[3072,128]{1,0:T(8,128)S(1)} %bitcast.6), channel_id=1, source_target_pairs={{0,4},{4,0},{1,5},{5,1},{2,6},{6,2},{3,7},{7,3},{8,12},{12,8},{9,1... | collective-permute-start | bytes 4718600 | tf_op jit(solution)/shard_map/ppermute | solution.py:267
  128.1 1.2 copy-start.7
  142.0 5.0 %collective-permute-start.11 = (f32[32,512]{1,0:T(8,128)}, f32[32,512]{1,0:T(8,128)S(1)}, u32[]{:S(2)}, u32[]{:S(2)}) collective-permute-start(f32[32,512]{1,0:T(8,128)} %get-tuple-element.30.a0), channel_id=1, source_target_pairs={{0,3},{1,0},{2,1},{3,2},{4,7},{5,4},{6,5},{7,6},{8,11},{9,8},{10,9... | collective-permute-start | bytes 196616 | tf_op jit(solution)/shard_map/ppermute | solution.py:229
  142.8 6.2 %collective-permute-start.10 = (f32[32,512]{1,0:T(8,128)}, f32[32,512]{1,0:T(8,128)S(1)}, u32[]{:S(2)}, u32[]{:S(2)}) collective-permute-start(f32[32,512]{1,0:T(8,128)} %get-tuple-element.30.a0), channel_id=1, source_target_pairs={{0,2},{1,3},{2,0},{3,1},{4,6},{5,7},{6,4},{7,5},{8,10},{9,11},{10,... | collective-permute-start | bytes 196616 | tf_op jit(solution)/shard_map/ppermute | solution.py:229
  144.5 5.7 %collective-permute-start.9 = (f32[32,512]{1,0:T(8,128)}, f32[32,512]{1,0:T(8,128)S(1)}, u32[]{:S(2)}, u32[]{:S(2)}) collective-permute-start(f32[32,512]{1,0:T(8,128)} %get-tuple-element.30.a0), channel_id=1, source_target_pairs={{0,1},{1,2},{2,3},{3,0},{4,5},{5,6},{6,7},{7,4},{8,9},{9,10},{10,1... | collective-permute-start | bytes 196616 | tf_op jit(solution)/shard_map/ppermute | solution.py:229
  147.0 3.2 %copy-start.11 = (f32[32,512]{1,0:T(8,128)}, f32[32,512]{1,0:T(8,128)S(1)}, u32[]{:S(2)}) copy-start(f32[32,512]{1,0:T(8,128)S(1)} %collective-permute-done.11.a3) | copy-start | bytes 196612
  149.0 1.2 copy-start.12
  150.2 0.6 copy-start.13
